TPU v7x, 32 devices: a whole 2x2x4 slice. The times are simulated.
32 devices in a mesh: dp: 8 (over z, y), head: 4 (over x, core).
Axes of the slice: x: 2, y: 2, z: 4, core: 2. Of those that a mesh axis runs over, the one named last changes fastest.
Arguments:
- tokens: bfloat16 [24576, 768], P(('dp', 'head')), may hold values from -15 to 15
- segment_ids: int32 [24576], P('dp'), may hold values from 0 to 189, as said below
- cotangent: bfloat16 [24576, 768], P(('dp', 'head')), may hold values from -6 to 6
- clip_norm: float32 [1], replicated, as said below
- master_qkv: float32 [768, 2304], P('dp'), may hold values from -0.21875 to 0.21875
- master_out: float32 [768, 768], P('dp'), may hold values from -0.875 to 0.875
- master_gu: float32 [768, 6144], P('dp'), may hold values from -0.72168784 to 0.72168784
- master_down: float32 [3072, 768], P('dp'), may hold values from -0.109375 to 0.109375
- master_vec: float32 [6, 768], P(None, 'dp')
- first_qkv: float32 [768, 2304], P('dp')
- first_out: float32 [768, 768], P('dp')
- first_gu: float32 [768, 6144], P('dp')
- first_down: float32 [3072, 768], P('dp')
- first_vec: float32 [6, 768], P(None, 'dp')
- second_qkv: float32 [768, 2304], P('dp'), as said below
- second_out: float32 [768, 768], P('dp'), as said below
- second_gu: float32 [768, 6144], P('dp'), as said below
- second_down: float32 [3072, 768], P('dp'), as said below
- second_vec: float32 [6, 768], P(None, 'dp'), as said below
Outputs:
- output: bfloat16 [24576, 768], P(('dp', 'head'))
- grad_input: float32 [24576, 768], P(('dp', 'head'))
- new_qkv: float32 [768, 2304], P('dp')
- moment1_qkv: float32 [768, 2304], P('dp')
- moment2_qkv: float32 [768, 2304], P('dp')
- copy_qkv: bfloat16 [768, 2304], P('dp')
- new_out: float32 [768, 768], P('dp')
- moment1_out: float32 [768, 768], P('dp')
- moment2_out: float32 [768, 768], P('dp')
- copy_out: bfloat16 [768, 768], P('dp')
- new_gu: float32 [768, 6144], P('dp')
- moment1_gu: float32 [768, 6144], P('dp')
- moment2_gu: float32 [768, 6144], P('dp')
- copy_gu: bfloat16 [768, 6144], P('dp')
- new_down: float32 [3072, 768], P('dp')
- moment1_down: float32 [3072, 768], P('dp')
- moment2_down: float32 [3072, 768], P('dp')
- copy_down: bfloat16 [3072, 768], P('dp')
- new_vec: float32 [6, 768], P(None, 'dp')
- moment1_vec: float32 [6, 768], P(None, 'dp')
- moment2_vec: float32 [6, 768], P(None, 'dp')
- copy_vec: bfloat16 [6, 768], P(None, 'dp')
- grad_norm: float32 [1], replicated
Inputs may be any that keep to these rules, and one draw needn't show every extreme that they name: `segment_ids`: ids never fall; each aligned block of 1024 tokens holds whole sequences of 128, 256 or 512 tokens, and no id appears in two blocks; block k's ids lie within 8 * k to 8 * k + 5. `clip_norm`: Positive. `second_qkv`: Positive. `second_out`: Positive. `second_gu`: Positive. `second_down`: Positive. `second_vec`: Positive.
All inputs are finite; a program needn't handle non-finite values.
Results may differ from a plain program's by a relative error of at most 0.019.
The roundings to bfloat16 on the way count: a program that leaves them out, or rounds other values in their place, can miss the bound.
Values may be sent and summed in bfloat16 or wider, within the bound.
No kernel may reach another device: no remote copies, remote signals or barrier semaphores. Data moves between devices by JAX's collectives and lax.ppermute only.
A program may use at most 192 MiB of HBM per device.

v0:
```python
import jax
import jax.numpy as jnp
import numpy as np
from jax import lax
from jax.sharding import PartitionSpec as P

HEADS = 12
HEAD_DIM = 64
PACK = 1024
SLOPES = [2.0 ** (-(level + 1)) for level in range(8)] + [
    2.0 ** (-(level + 0.5)) for level in range(4)
]
LN_EPS = 1e-05
BETA_ONE = 0.9
BETA_TWO = 0.999
ADAM_EPS = 1e-08
CORR_ONE = 1.0 - 0.9**10
CORR_TWO = 1.0 - 0.999**10
RATE_MAT = 0.05
RATE_VEC = 0.5
DECAY_MAT = 0.01


def layer_norm(hidden, gain_vec, shift_vec):
    center = hidden - jnp.mean(hidden, axis=-1, keepdims=True)
    spread = jnp.mean(center * center, axis=-1, keepdims=True)
    return center * lax.rsqrt(spread + LN_EPS) * gain_vec + shift_vec


def gating(joined):
    half_width = joined.shape[-1] // 2
    return jax.nn.gelu(joined[:, :half_width], approximate=False) * joined[:, half_width:]


def contract_rows(left_rows, right_rows):
    return lax.dot_general(
        left_rows, right_rows, (((0,), (0,)), ((), ())), preferred_element_type=jnp.float32
    )


def times_transposed(left_rows, weight):
    return lax.dot_general(
        left_rows, weight, (((1,), (1,)), ((), ())), preferred_element_type=jnp.float32
    )


def adam_update(master, first_mom, second, grad_term, factor, step_rate, decay_rate):
    clipped = grad_term * factor
    first_new = BETA_ONE * first_mom + (1.0 - BETA_ONE) * clipped
    second_new = BETA_TWO * second + (1.0 - BETA_TWO) * clipped * clipped
    direction = first_new / CORR_ONE / (jnp.sqrt(second_new / CORR_TWO) + ADAM_EPS)
    master_new = master - step_rate * (direction + decay_rate * master)
    return (master_new, first_new, second_new, master_new.astype(jnp.bfloat16))


def pack_scores(queries, keys_part, seg_pack, slopes_local, score_scale):
    scores = (
        jnp.einsum("qhd,khd->hqk", queries, keys_part, preferred_element_type=jnp.float32)
        * score_scale
    )
    positions = jnp.arange(seg_pack.shape[0]).astype(jnp.float32)
    distance = jnp.abs(positions[:, None] - positions[None, :])
    same_seq = seg_pack[:, None] == seg_pack[None, :]
    return jnp.where(
        same_seq[None], scores - slopes_local[:, None, None] * distance[None], -1000000000.0
    )


def body(
    tokens,
    segment_ids,
    cotangent,
    clip_norm,
    master_qkv,
    master_out,
    master_gu,
    master_down,
    master_vec,
    first_qkv,
    first_out,
    first_gu,
    first_down,
    first_vec,
    second_qkv,
    second_out,
    second_gu,
    second_down,
    second_vec,
):
    groups = lax.axis_size("head")
    heads_local = HEADS // groups
    group_width = heads_local * HEAD_DIM
    tok_rows = tokens.shape[0]
    model_width = tokens.shape[1]
    score_scale = HEAD_DIM ** (-0.5)
    low_qkv = master_qkv.astype(jnp.bfloat16)
    low_out = master_out.astype(jnp.bfloat16)
    low_gu = master_gu.astype(jnp.bfloat16)
    low_down = master_down.astype(jnp.bfloat16)
    low_vec = master_vec.astype(jnp.bfloat16)
    full_qkv, full_out, full_gu, full_down, full_vec = (
        lax.all_gather(low_qkv, "dp", axis=0, tiled=True),
        lax.all_gather(low_out, "dp", axis=0, tiled=True),
        lax.all_gather(low_gu, "dp", axis=0, tiled=True),
        lax.all_gather(low_down, "dp", axis=0, tiled=True),
        lax.all_gather(low_vec, "dp", axis=1, tiled=True),
    )
    vectors = full_vec.astype(jnp.float32)
    slopes_local = lax.dynamic_slice_in_dim(
        jnp.asarray(np.array(SLOPES), jnp.float32),
        lax.axis_index("head") * heads_local,
        heads_local,
    )
    joined = jnp.dot(tokens, full_qkv, preferred_element_type=jnp.float32).astype(jnp.bfloat16)
    regrouped = lax.all_to_all(
        joined.reshape(tok_rows, 3, groups, group_width),
        "head",
        split_axis=2,
        concat_axis=0,
        tiled=True,
    )
    group_rows = regrouped.shape[0]
    pack_count = group_rows // PACK
    by_pack = regrouped.reshape(pack_count, PACK, 3, heads_local, HEAD_DIM)
    seg_packs = segment_ids.reshape(pack_count, PACK)

    def forward_pack(pieces):
        pack_block, seg_pack = pieces
        scores = pack_scores(
            pack_block[:, 0], pack_block[:, 1], seg_pack, slopes_local, score_scale
        )
        row_peak = jnp.max(scores, axis=-1, keepdims=True)
        exp_terms = jnp.exp(scores - row_peak)
        row_total = jnp.sum(exp_terms, axis=-1, keepdims=True)
        soft_weights = (exp_terms / row_total).astype(jnp.bfloat16)
        context = jnp.einsum(
            "hqk,khd->qhd", soft_weights, pack_block[:, 2], preferred_element_type=jnp.float32
        )
        return (
            context.astype(jnp.bfloat16).reshape(PACK, group_width),
            (row_peak + jnp.log(row_total))[..., 0],
        )

    context_packs, log_totals = lax.map(forward_pack, (by_pack, seg_packs))
    context_back = lax.all_to_all(
        context_packs.reshape(group_rows, 1, group_width),
        "head",
        split_axis=0,
        concat_axis=1,
        tiled=True,
    )
    context_rows = context_back.reshape(tok_rows, model_width)
    inputs = tokens.astype(jnp.float32)
    attn_out = jnp.dot(context_rows, full_out, preferred_element_type=jnp.float32)
    first_sum = inputs + attn_out + vectors[4]
    normed_one, norm_one_pull = jax.vjp(layer_norm, first_sum, vectors[0], vectors[1])
    normed_low = normed_one.astype(jnp.bfloat16)
    gate_up = jnp.dot(normed_low, full_gu, preferred_element_type=jnp.float32)
    hidden_full, gating_pull = jax.vjp(gating, gate_up)
    hidden_low = hidden_full.astype(jnp.bfloat16)
    ffn_out = jnp.dot(hidden_low, full_down, preferred_element_type=jnp.float32)
    second_sum = normed_one + ffn_out + vectors[5]
    result, norm_two_pull = jax.vjp(layer_norm, second_sum, vectors[2], vectors[3])
    grad_second, grad_gain_two, grad_shift_two = norm_two_pull(cotangent.astype(jnp.float32))
    grad_bias_down = jnp.sum(grad_second, axis=0)
    grad_ffn_low = grad_second.astype(jnp.bfloat16)
    grad_down = contract_rows(hidden_low, grad_ffn_low)
    grad_hidden = times_transposed(grad_ffn_low, full_down)
    (grad_joined_full,) = gating_pull(grad_hidden)
    grad_gate_up = grad_joined_full.astype(jnp.bfloat16)
    grad_gu = contract_rows(normed_low, grad_gate_up)
    grad_normed = grad_second + times_transposed(grad_gate_up, full_gu)
    grad_first, grad_gain_one, grad_shift_one = norm_one_pull(grad_normed)
    grad_bias_out = jnp.sum(grad_first, axis=0)
    grad_attn_low = grad_first.astype(jnp.bfloat16)
    grad_out = contract_rows(context_rows, grad_attn_low)
    grad_context = times_transposed(grad_attn_low, full_out).astype(jnp.bfloat16)
    grad_context_group = lax.all_to_all(
        grad_context.reshape(tok_rows, groups, group_width),
        "head",
        split_axis=1,
        concat_axis=0,
        tiled=True,
    )
    grad_packs = grad_context_group.reshape(pack_count, PACK, heads_local, HEAD_DIM)

    def backward_pack(pieces):
        pack_block, seg_pack, log_total, grad_ctx = pieces
        queries = pack_block[:, 0]
        keys_part = pack_block[:, 1]
        values_part = pack_block[:, 2]
        scores = pack_scores(queries, keys_part, seg_pack, slopes_local, score_scale)
        soft_full = jnp.exp(scores - log_total[..., None])
        grad_soft = jnp.einsum(
            "qhd,khd->hqk", grad_ctx, values_part, preferred_element_type=jnp.float32
        )
        grad_values = jnp.einsum(
            "hqk,qhd->khd",
            soft_full.astype(jnp.bfloat16),
            grad_ctx,
            preferred_element_type=jnp.float32,
        )
        row_inner = jnp.sum(soft_full * grad_soft, axis=-1, keepdims=True)
        grad_scores = (soft_full * (grad_soft - row_inner)).astype(jnp.bfloat16)
        grad_queries = (
            jnp.einsum("hqk,khd->qhd", grad_scores, keys_part, preferred_element_type=jnp.float32)
            * score_scale
        )
        grad_keys = (
            jnp.einsum("hqk,qhd->khd", grad_scores, queries, preferred_element_type=jnp.float32)
            * score_scale
        )
        stacked = jnp.stack((grad_queries, grad_keys, grad_values), axis=1).astype(jnp.bfloat16)
        return stacked.reshape(PACK, 3, group_width)

    grad_blocks = lax.map(backward_pack, (by_pack, seg_packs, log_totals, grad_packs))
    grad_joined = lax.all_to_all(
        grad_blocks.reshape(group_rows, 3, 1, group_width),
        "head",
        split_axis=0,
        concat_axis=2,
        tiled=True,
    )
    grad_joined_rows = grad_joined.reshape(tok_rows, 3 * model_width)
    grad_qkv = contract_rows(tokens, grad_joined_rows)
    grad_input = grad_first + times_transposed(grad_joined_rows, full_qkv)
    grad_vec = jnp.stack(
        (
            grad_gain_one,
            grad_shift_one,
            grad_gain_two,
            grad_shift_two,
            grad_bias_out,
            grad_bias_down,
        )
    )
    shard_qkv, shard_out, shard_gu, shard_down, shard_vec = (
        lax.psum_scatter(grad_qkv, "dp", scatter_dimension=0, tiled=True),
        lax.psum_scatter(grad_out, "dp", scatter_dimension=0, tiled=True),
        lax.psum_scatter(grad_gu, "dp", scatter_dimension=0, tiled=True),
        lax.psum_scatter(grad_down, "dp", scatter_dimension=0, tiled=True),
        lax.psum_scatter(grad_vec, "dp", scatter_dimension=1, tiled=True),
    )
    shards = (
        lax.psum(shard_qkv.astype(jnp.bfloat16), "head").astype(jnp.float32),
        lax.psum(shard_out.astype(jnp.bfloat16), "head").astype(jnp.float32),
        lax.psum(shard_gu.astype(jnp.bfloat16), "head").astype(jnp.float32),
        lax.psum(shard_down.astype(jnp.bfloat16), "head").astype(jnp.float32),
        lax.psum(shard_vec.astype(jnp.bfloat16), "head").astype(jnp.float32),
    )
    squares = jnp.float32(0.0)
    for shard_piece in shards:
        squares = squares + jnp.sum(shard_piece * shard_piece)
    grad_norm = jnp.sqrt(lax.psum(squares, "dp"))
    factor = jnp.minimum(1.0, clip_norm[0] / grad_norm)
    up_qkv = adam_update(master_qkv, first_qkv, second_qkv, shards[0], factor, RATE_MAT, DECAY_MAT)
    up_out = adam_update(master_out, first_out, second_out, shards[1], factor, RATE_MAT, DECAY_MAT)
    up_gu = adam_update(master_gu, first_gu, second_gu, shards[2], factor, RATE_MAT, DECAY_MAT)
    up_down = adam_update(
        master_down, first_down, second_down, shards[3], factor, RATE_MAT, DECAY_MAT
    )
    up_vec = adam_update(master_vec, first_vec, second_vec, shards[4], factor, RATE_VEC, 0.0)
    return (
        result.astype(jnp.bfloat16),
        grad_input,
        up_qkv[0],
        up_qkv[1],
        up_qkv[2],
        up_qkv[3],
        up_out[0],
        up_out[1],
        up_out[2],
        up_out[3],
        up_gu[0],
        up_gu[1],
        up_gu[2],
        up_gu[3],
        up_down[0],
        up_down[1],
        up_down[2],
        up_down[3],
        up_vec[0],
        up_vec[1],
        up_vec[2],
        up_vec[3],
        grad_norm.reshape(1),
    )


def solution(mesh):
    in_specs = (
        P(("dp", "head"), None),
        P("dp"),
        P(("dp", "head"), None),
        P(),
        P("dp", None),
        P("dp", None),
        P("dp", None),
        P("dp", None),
        P(None, "dp"),
        P("dp", None),
        P("dp", None),
        P("dp", None),
        P("dp", None),
        P(None, "dp"),
        P("dp", None),
        P("dp", None),
        P("dp", None),
        P("dp", None),
        P(None, "dp"),
    )
    out_specs = (
        P(("dp", "head"), None),
        P(("dp", "head"), None),
        P("dp", None),
        P("dp", None),
        P("dp", None),
        P("dp", None),
        P("dp", None),
        P("dp", None),
        P("dp", None),
        P("dp", None),
        P("dp", None),
        P("dp", None),
        P("dp", None),
        P("dp", None),
        P("dp", None),
        P("dp", None),
        P("dp", None),
        P("dp", None),
        P(None, "dp"),
        P(None, "dp"),
        P(None, "dp"),
        P(None, "dp"),
        P(),
    )
    return jax.shard_map(body, mesh=mesh, in_specs=in_specs, out_specs=out_specs, check_vma=False)
```

profile of v0, /device:TPU:0, one launch (start us, length us, event | category | flops | bytes accessed | tf_op | source)
XLA Modules:
  0.0 1466.3 jit_solution(240032955310916540)
XLA Ops:
  9.2 69.5 %all-gather.6.cloned.1.call-done = bf16[768,2304]{1,0:T(8,128)(2,1)} async-done(((bf16[96,2304]{1,0:T(8,128)(2,1)}), bf16[768,2304]{1,0:T(8,128)(2,1)}) %all-gather.6.cloned.1.call-update) | async-done | bytes 3538960 | tf_op jit(solution)/shard_map/all_gather | solution.py:102
  78.7 7.0 convolution_convert_fusion
  85.7 4.5 copy.129
  92.3 3.7 all-to-all-start
  102.7 34.4 %all-to-all-done = bf16[768,3,4,192]{0,3,1,2:T(8,128)(2,1)S(1)} async-done(((bf16[768,3,4,192]{0,3,1,2:T(8,128)(2,1)}), bf16[768,3,4,192]{0,3,1,2:T(8,128)(2,1)S(1)}, u32[]{:S(2)}, u32[]{:S(2)}) %all-to-all-start) | async-done | bytes 3538976 | tf_op jit(solution)/shard_map/all_to_all | solution.py:115
  137.1 4.5 copy.131
  141.6 10.9 reshape.363
  152.5 3.7 copy.132
  156.2 45.1 %while.22 = (s32[]{:T(128)}, bf16[3,1024,192]{1,2,0:T(8,128)(2,1)}, f32[3,3,1024]{2,1,0:T(4,128)}, bf16[3,1024,3,3,64]{1,4,3,2,0:T(8,128)(2,1)S(1)}, s32[3,1024]{1,0:T(4,128)S(1)}, /*index=5*/f32[3]{0:T(128)}, s32[]{:T(128)}) while((s32[]{:T(128)}, bf16[3,1024,192]{1,2,0:T(8,128)(2,1)}, f32[3,3,1024]{2,1,0:T(4,128)}, ...), condition=%wide.region_3.4_spmd, body=%wide.region_0.3_spmd.sunk | while | flops 865269760 | bytes 63571132 | solution.py:144
  157.4 3.4 fusion.115
  160.9 3.9 fusion.116
  164.8 5.1 fusion.117
  172.5 3.4 fusion.115
  175.9 3.9 fusion.116
  179.8 5.1 fusion.117
  187.5 3.5 fusion.115
  190.9 3.9 fusion.116
  194.8 5.1 fusion.117
  203.8 10.0 reshape.379
  214.4 19.5 %reduce.12 = bf16[3072,192]{1,0:T(8,128)(2,1)} reduce(bf16[3072,1,192]{2,1,0:T(2,128)(2,1)} %reshape.379, bf16[]{:T(256)} %broadcast.241), dimensions={1}, to_apply=%reshape.379.reduce_sub_computation | reduce | bytes 2359298 | tf_op jit(solution)/shard_map/reshape | solution.py:146
  233.9 4.4 reshape.390
  238.2 4.3 all-to-all-start.1
  249.5 26.2 %all-gather = bf16[8,96,6]{1,2,0:T(8,128)(2,1)S(1)} all-gather(bf16[1,96,6]{1,2,0:T(8,128)(2,1)S(1)} %convert_bitcast_fusion), channel_id=1, replica_groups=mesh['dp'=8,'head'=4] {'dp'}, dimensions={0}, use_global_device_ids=true | all-gather | bytes 10368 | tf_op jit(solution)/shard_map/all_gather | solution.py:106
  279.3 4.8 reshape.391
  284.1 7.3 copy.135
  291.4 3.5 all_to_all.48
  302.8 11.6 fusion.63
  314.4 6.8 copy-done
  321.2 21.9 %multiply_convert_fusion.1 = (bf16[768,3072]{1,0:T(8,128)(2,1)}, f32[768,3072]{1,0:T(8,128)}) fusion(f32[768,6144]{1,0:T(8,128)S(1)} %fusion.63), kind=kLoop, calls=%fused_computation.51 | loop fusion | flops 155713536 | bytes 33030144 | tf_op jit(solution)/shard_map/convert_element_type | solution.py:160
  343.1 17.3 %all-gather.12.cloned.1.call-done = bf16[3072,768]{1,0:T(8,128)(2,1)} async-done(((bf16[384,768]{1,0:T(8,128)(2,1)}), bf16[3072,768]{1,0:T(8,128)(2,1)}) %all-gather.12.cloned.1.call-update) | async-done | bytes 4718608 | tf_op jit(solution)/shard_map/all_gather | solution.py:105
  360.3 9.0 fusion.84
  374.9 18.9 %fusion.28 = (f32[768,3072]{1,0:T(8,128)}, f32[768,3072]{1,0:T(8,128)}) fusion(f32[768,3072]{1,0:T(8,128)} %get-tuple-element.294, f32[768,6144]{1,0:T(8,128)} %copy-done, bf16[3072,768]{1,0:T(8,128)(2,1)} %all-gather.12.cloned.1.call-done, f32[768,768]{0,1:T(8,128)} %get-tuple-element.292, f32[768]{0:T(1024)S(1)} %negate_multiply_fusion.2), kind=kOutput, calls=%fused_computation.75 | convolution fusion | flops 3662807040 | bytes 54266880 | tf_op jit(solution)/shard_map/dot_general | solution.py:42
  393.8 19.8 %multiply_reduce_fusion.1 = (f32[768]{0:T(1024)}, f32[768]{0:T(1024)}, f32[768]{0:T(1024)}, f32[768,768]{0,1:T(8,128)}) fusion(f32[768,768]{0,1:T(8,128)} %copy-done.3, f32[768]{0:T(1024)S(1)} %fusion.58, f32[768]{0:T(1024)S(1)} %broadcast_multiply_fusion.1, f32[768]{0:T(1024)S(1)} %get-tuple-element.237, ...), kind=kOutput, calls=%fused_computation.87 | convolution fusion | flops 7263089664 | bytes 35410944 | tf_op jit(solution)/shard_map/dot_general | solution.py:42
  419.6 4.3 all-to-all-start.2
  424.0 4.6 fusion.49
  428.6 11.2 all-to-all-done.2
  443.0 4.5 reshape.368
  450.5 95.2 %while.23 = (s32[]{:T(128)}, bf16[3,1024,3,192]{1,3,2,0:T(8,128)(2,1)}, bf16[3,1024,3,3,64]{1,4,3,2,0:T(8,128)(2,1)S(1)}, s32[3,1024]{1,0:T(4,128)}, f32[3]{0:T(...) while((s32[]{:T(128)}, bf16[3,1024,3,192]{1,3,2,0:T(8,128)(2,1)}, ...), condition=%wide.region_14.15_spmd, body=%wide.region_12.14_spmd.sunk | while | flops 2055534592 | bytes 141906608 | solution.py:216
  456.2 8.2 multiply_reduce_fusion.6
  464.4 6.9 fusion.124
  471.3 6.6 multiply_convert_fusion.3
  488.0 8.2 multiply_reduce_fusion.6
  496.2 6.7 fusion.124
  502.9 6.6 multiply_convert_fusion.3
  519.7 8.2 multiply_reduce_fusion.6
  527.9 6.7 fusion.124
  534.6 6.6 multiply_convert_fusion.3
  545.6 9.8 copy.165
  555.5 77.7 %all_to_all.60 = bf16[3072,3,1,192]{3,1,2,0:T(4,128)(2,1)} all-to-all(bf16[3072,3,1,192]{3,1,2,0:T(4,128)(2,1)} %bitcast.155), channel_id=1, replica_groups=mesh['dp'=8,'head'=4] {'head'}, dimensions={0} | all-to-all | bytes 7077888 | tf_op jit(solution)/shard_map/all_to_all | solution.py:217
  633.2 10.5 copy.166
  646.1 4.9 convolution_bitcast_fusion
  651.0 8.0 copy.167
  660.7 8.8 fusion.47
  671.2 20.7 %fusion.40 = f32[768,6144]{1,0:T(8,128)} fusion(f32[768,3072]{1,0:T(8,128)} %get-tuple-element.300, f32[768,3072]{1,0:T(8,128)} %get-tuple-element.299, f32[768,768]{0,1:T(8,128)S(1)} %copy-done.4, f32[768]{0:T(1024)S(1)} %copy-done.31, f32[768]{0:T(1024)S(1)} %copy-done.29, f32[768]{0:T(1024)S(1)} %copy-done.27, f32[768]{0:T(1024)S(1)} %copy-done.25), kind=kOutput, calls=%fused_computation.111 | convolution fusion | flops 7260143616 | bytes 40120320 | tf_op jit(solution)/shard_map/dot_general | solution.py:36
  697.4 88.2 %reduce-scatter.16.cloned.1.call-done = f32[96,2304]{1,0:T(8,128)} async-done(((f32[768,2304]{1,0:T(8,128)}), f32[96,2304]{1,0:T(8,128)}) %reduce-scatter.16.cloned.1.call-update) | async-done | bytes 884752
  787.7 164.3 %reduce-scatter.14.cloned.1.call-done = f32[384,768]{1,0:T(8,128)} async-done(((f32[3072,768]{1,0:T(8,128)}), f32[384,768]{1,0:T(8,128)}) %reduce-scatter.14.cloned.1.call-update) | async-done | bytes 1179664 | tf_op jit(solution)/shard_map/reduce_scatter | solution.py:241
  954.2 314.8 %reduce-scatter.12.cloned.1.call-done = f32[96,6144]{1,0:T(8,128)} async-done(((f32[768,6144]{1,0:T(8,128)}), f32[96,6144]{1,0:T(8,128)}) %reduce-scatter.12.cloned.1.call-update) | async-done | bytes 2359312 | tf_op jit(solution)/shard_map/reduce_scatter | solution.py:240
  1280.5 53.2 %reduce-scatter.18.cloned.1.call-done = f32[96,6]{1,0:T(8,128)} async-done(((f32[768,6]{1,0:T(8,128)}), f32[96,6]{1,0:T(8,128)}) %reduce-scatter.18.cloned.1.call-update) | async-done | bytes 2320
  1334.5 5.8 psum.46
  1341.0 7.9 add_add_fusion.4
  1348.8 47.1 %all-reduce.5.cloned.1.call-done = (bf16[96,2304]{0,1:T(8,128)(2,1)}, bf16[96,768]{1,0:T(8,128)(2,1)}, bf16[96,6144]{1,0:T(8,128)(2,1)}, bf16[384,768]{1,0:T(8,128)(2,1)}) async-done(((bf16[96,2304]{0,1:T(8,128)(2,1)}, bf16[96,768]{1,0:T(8,128)(2,1)}, bf16[96,6144]{1,0:T(8,128)(2,1)}, bf16[384,768]{1,0:T(8,128)(2,1)}), (bf16[96,2304]{0,1:T(8,128)(2,1)}, bf16[96,768]{1,0:T(8,128)(2,1)}, ...) | async-done | bytes 2359312 | tf_op jit(solution)/shard_map/psum | solution.py:245
  1410.4 21.8 %psum.47 = f32[]{:T(128)} all-reduce(f32[]{:T(128)S(6)} %add.231), channel_id=1, replica_groups=mesh['dp'=8,'head'=4] {'dp'}, use_global_device_ids=true, to_apply=%region_36.37 | all-reduce | flops 1 | bytes 8 | tf_op jit(solution)/shard_map/psum | solution.py:254
  1433.0 3.7 fusion.77
  1447.7 7.1 fusion.71
  (259 shorter events, 141.0 us)
Async XLA Ops:
  7.2 71.5 %all-gather.6.cloned.1.call-start = ((), (), s32[]{:S(2)}) async-start(), calls=%async_computation.9 | async-start | bytes 3981312 | tf_op jit(solution)/shard_map/all_gather | solution.py:102
  92.3 44.9 %all-to-all-start = ((bf16[768,3,4,192]{0,3,1,2:T(8,128)(2,1)}), bf16[768,3,4,192]{0,3,1,2:T(8,128)(2,1)S(1)}, u32[]{:S(2)}, u32[]{:S(2)}) async-start(bf16[768,3,4,192]{0,3,1,2:T(8,128)(2,1)} %copy.130), calls=%async_computation | async-start | bytes 7077888 | tf_op jit(solution)/shard_map/all_to_all | solution.py:115
  96.0 201.2 %all-gather.8.cloned.1.call-start = ((), (), s32[]{:S(2)}) async-start(), calls=%async_computation.10 | async-start | bytes 1327104 | tf_op jit(solution)/shard_map/all_gather | solution.py:103
  97.7 205.1 %all-gather.10.cloned.1.call-start = ((), (), s32[]{:S(2)}) async-start(), calls=%async_computation.11 | async-start | bytes 10616832 | tf_op jit(solution)/shard_map/all_gather | solution.py:104
  156.6 0.8 copy-start.33
  201.3 12.5 copy-start.32
  238.2 41.1 %all-to-all-start.1 = ((bf16[4,2,73728]{2,1,0:T(2,128)(2,1)}), bf16[4,2,73728]{2,1,0:T(2,128)(2,1)}, u32[]{:S(2)}, u32[]{:S(2)}) async-start(bf16[4,2,73728]{2,1,0:T(2,128)(2,1)} %reshape.390), calls=%async_computation.1 | async-start | bytes 2359296 | tf_op jit(solution)/shard_map/all_to_all | solution.py:145
  242.5 117.8 %all-gather.12.cloned.1.call-start = ((), (), s32[]{:S(2)}) async-start(), calls=%async_computation.12 | async-start | bytes 5308416 | tf_op jit(solution)/shard_map/all_gather | solution.py:105
  244.7 4.8 copy-start.45
  279.3 81.0 %copy-start.30 = (f32[768]{0:T(1024)}, f32[768]{0:T(1024)S(1)}, u32[]{:S(2)}) copy-start(f32[768]{0:T(1024)S(1)} %get-tuple-element.236) | copy-start | bytes 9220
  279.3 135.0 %copy-start.28 = (f32[768]{0:T(1024)}, f32[768]{0:T(1024)S(1)}, u32[]{:S(2)}) copy-start(f32[768]{0:T(1024)S(1)} %get-tuple-element.237) | copy-start | bytes 9220
  300.5 1.4 copy-start.3
  300.5 113.8 %copy-start.24 = (f32[768]{0:T(1024)}, f32[768]{0:T(1024)S(1)}, u32[]{:S(2)}) copy-start(f32[768]{0:T(1024)S(1)} %broadcast_multiply_fusion.1) | copy-start | bytes 9220
  302.8 111.5 %copy-start.26 = (f32[768]{0:T(1024)}, f32[768]{0:T(1024)S(1)}, u32[]{:S(2)}) copy-start(f32[768]{0:T(1024)S(1)} %fusion.58) | copy-start | bytes 9220
  314.4 6.8 copy-start
  369.3 1.3 copy-start.5
  369.3 1.3 copy-start.35
  369.6 2.6 copy-start.44
  374.9 18.9 %copy-start.42 = (f32[768]{0:T(1024)}, f32[768]{0:T(1024)S(1)}, u32[]{:S(2)}) copy-start(f32[768]{0:T(1024)S(1)} %negate_multiply_fusion.2) | copy-start | bytes 9220
  393.8 19.8 %copy-start.37 = (f32[768]{0:T(1024)S(1)}, f32[768]{0:T(1024)}, u32[]{:S(2)}) copy-start(f32[768]{0:T(1024)} %copy-done.36) | copy-start | bytes 9220
  414.3 3.1 copy-start.51
  417.4 2.2 copy-start.7
  417.5 6.5 copy-start.40
  419.6 20.2 %all-to-all-start.2 = ((bf16[768,4,192]{0,2,1:T(8,128)(2,1)}), bf16[768,4,192]{0,2,1:T(8,128)(2,1)}, u32[]{:S(2)}, u32[]{:S(2)}) async-start(bf16[768,4,192]{0,2,1:T(8,128)(2,1)} %bitcast.167), calls=%async_computation.2 | async-start | bytes 2359296 | tf_op jit(solution)/shard_map/all_to_all | solution.py:178
  423.9 271.8 %reduce-scatter.10.cloned.1.call-start = ((), (), s32[]{:S(2)}) async-start(), calls=%async_computation.13 | async-start | bytes 2654208 | tf_op jit(solution)/shard_map/reduce_scatter | solution.py:239
  428.6 357.0 %reduce-scatter.16.cloned.1.call-start = ((), (), s32[]{:S(2)}) async-start(), calls=%async_computation.16 | async-start | bytes 7962624
  443.0 7.4 copy-start.34
  450.5 3.2 copy-start.1
  479.9 2.3 copy-start.2
  482.2 3.2 copy-start.1
  511.6 2.4 copy-start.2
  513.9 3.2 copy-start.1
  543.3 2.4 copy-start.2
  643.7 2.4 copy-start.21
  644.2 1.9 copy-start.18
  659.1 1.7 copy-start.9
  659.1 1.7 copy-start.43
  659.1 293.0 %reduce-scatter.14.cloned.1.call-start = ((), (), s32[]{:S(2)}) async-start(), calls=%async_computation.15 | async-start | bytes 10616832 | tf_op jit(solution)/shard_map/reduce_scatter | solution.py:241
  669.5 1.7 copy-start.4
  669.5 1.7 copy-start.25
  669.5 1.7 copy-start.27
  669.5 1.7 copy-start.29
  669.5 1.7 copy-start.31
  669.6 599.4 %reduce-scatter.12.cloned.1.call-start = ((), (), s32[]{:S(2)}) async-start(), calls=%async_computation.14 | async-start | bytes 21233664 | tf_op jit(solution)/shard_map/reduce_scatter | solution.py:240
  691.9 1.7 copy-start.8
  691.9 1.7 copy-start.41
  692.0 641.7 %reduce-scatter.18.cloned.1.call-start = ((), (), s32[]{:S(2)}) async-start(), calls=%async_computation.17 | async-start | bytes 442368
  692.0 2.4 copy-start.10
  695.6 700.2 %all-reduce.5.cloned.1.call-start = ((), (), s32[]{:S(2)}) async-start(), calls=%async_computation.18 | async-start | bytes 5013504 | tf_op jit(solution)/shard_map/psum | solution.py:245
  954.2 317.6 %copy-start.19 = (f32[96,2304]{1,0:T(8,128)S(1)}, f32[96,2304]{1,0:T(8,128)}, u32[]{:S(2)}) copy-start(f32[96,2304]{1,0:T(8,128)} %param.28) | copy-start | bytes 2654212
  1273.2 5.9 copy-start.13
  1407.1 25.8 %copy-start.14 = (f32[96,2304]{0,1:T(8,128)S(1)}, f32[96,2304]{0,1:T(8,128)}, u32[]{:S(2)}) copy-start(f32[96,2304]{0,1:T(8,128)} %copy.151) | copy-start | bytes 2654212
  1407.2 25.8 %copy-start.15 = (f32[96,2304]{0,1:T(8,128)S(1)}, f32[96,2304]{0,1:T(8,128)}, u32[]{:S(2)}) copy-start(f32[96,2304]{0,1:T(8,128)} %copy.148) | copy-start | bytes 2654212
  1407.2 25.8 %copy-start.16 = (f32[96,2304]{0,1:T(8,128)S(1)}, f32[96,2304]{0,1:T(8,128)}, u32[]{:S(2)}) copy-start(f32[96,2304]{0,1:T(8,128)} %copy.149) | copy-start | bytes 2654212
  1436.7 2.6 copy-start.17
  1440.6 7.1 copy-start.6
  1440.6 7.1 copy-start.11
  1447.7 7.2 copy-start.12
  1447.7 7.2 copy-start.20
  1447.7 7.1 copy-start.22
  1447.7 7.1 copy-start.23
  1454.8 2.7 copy-start.46
  1454.9 2.7 copy-start.47
  1454.9 2.7 copy-start.48
  (7 other events, 5.1 us)
Sparse Core Ops, SparseCore 0:
  10.8 67.8 all-gather.5
  99.6 40.1 all-gather.7
  142.5 136.8 all-gather.9
  282.0 78.2 all-gather.11
  428.7 67.6 reduce-scatter.9
  659.2 126.2 reduce-scatter.15
  789.5 162.4 reduce-scatter.13
  956.4 312.4 reduce-scatter.11
  1273.1 60.4 reduce-scatter.17
  1338.0 57.7 all-reduce.4
where the time goes:
time: 1480 us; the launch traced here: 1470 us
  waiting for transfers between devices  800 us (54%)
  matrix products  208 us (14%)
  local copies, waits for them, and re-layouts  159 us (11%)
  other arithmetic  134 us (9%)
  blocking collectives  132 us (9%)
  between operations  20.8 us (1%)
    reduce_scatter x1, waiting for transfers between devices, body(): lax.psum_scatter(grad_gu, 'dp', scatter_dimension=0, tiled=True)  315 us
    reduce_scatter x1, waiting for transfers between devices, body(): lax.psum_scatter(grad_down, 'dp', scatter_dimension=0, tiled=True)  164 us
    unnamed x12, waiting for transfers between devices  141 us
    all_to_all x1, blocking collectives, body(): lax.all_to_all(grad_blocks.reshape(group_rows, 3, 1, group_width), 'head'...  77.7 us
    all_gather x1, waiting for transfers between devices, body(): lax.all_gather(low_qkv, 'dp', axis=0, tiled=True)  69.5 us
    unnamed x115, local copies, waits for them, and re-layouts  62.8 us
    dot_general x4, matrix products, times_transposed(): lax.dot_general(left_rows, weight, (((1,), (1,)), ((), ())), preferred_el...  48.7 us
    psum x1, waiting for transfers between devices, body(): lax.psum(shard_qkv.astype(jnp.bfloat16), 'head').astype(jnp.float32)  47.1 us
  transfers between devices with their start and end apart: 13, of which 9 were waited for; matrix products, arithmetic and copies ran while one was open for 25% of the time, Pallas kernels for 0%

commit v1 on v0

--- a/solution.py
+++ b/solution.py
@@ -19,6 +19,11 @@
 RATE_MAT = 0.05
 RATE_VEC = 0.5
 DECAY_MAT = 0.01
+
+
+def summed_here(x, name):
+    pieces = lax.all_gather(x, name)
+    return jnp.sum(pieces, axis=0)
 
 
 def layer_norm(hidden, gain_vec, shift_vec):
@@ -242,7 +247,7 @@
         lax.psum_scatter(grad_vec, "dp", scatter_dimension=1, tiled=True),
     )
     shards = (
-        lax.psum(shard_qkv.astype(jnp.bfloat16), "head").astype(jnp.float32),
+        summed_here(shard_qkv.astype(jnp.bfloat16), "head").astype(jnp.float32),
         lax.psum(shard_out.astype(jnp.bfloat16), "head").astype(jnp.float32),
         lax.psum(shard_gu.astype(jnp.bfloat16), "head").astype(jnp.float32),
         lax.psum(shard_down.astype(jnp.bfloat16), "head").astype(jnp.float32),

time: 1480 us -> 1550 us (1.047)
  waiting for transfers between devices: 800 us -> 889 us
    reduce_scatter x0 -> x1, waiting for transfers between devices: none -> 84.4 us  [body(): lax.psum_scatter(grad_qkv, 'dp', scatter_dimension=0, tiled=True)]
    unnamed x12, waiting for transfers between devices: 141 us -> 60.5 us
    reduce_scatter x1, waiting for transfers between devices: 0.02 us -> 65.3 us  [body(): lax.psum_scatter(grad_out, 'dp', scatter_dimension=0, tiled=True)]
    unnamed x115, local copies, waits for them, and re-layouts: 62.8 us -> 44.7 us
  transfers between devices with their start and end apart: 13 -> 14, of which waited for: 9 -> 11; matrix products, arithmetic and copies ran while one was open for 25% -> 15% of each run, Pallas kernels for 0% -> 0%
where the time goes in v1:
time: 1550 us; the launch traced here: 1540 us
  waiting for transfers between devices  889 us (57%)
  matrix products  206 us (13%)
  local copies, waits for them, and re-layouts  144 us (9%)
  other arithmetic  133 us (9%)
  blocking collectives  132 us (9%)
  between operations  20.4 us (1%)
    reduce_scatter x1, waiting for transfers between devices, body(): lax.psum_scatter(grad_gu, 'dp', scatter_dimension=0, tiled=True)  315 us
    reduce_scatter x1, waiting for transfers between devices, body(): lax.psum_scatter(grad_down, 'dp', scatter_dimension=0, tiled=True)  165 us
    reduce_scatter x1, waiting for transfers between devices, body(): lax.psum_scatter(grad_qkv, 'dp', scatter_dimension=0, tiled=True)  84.4 us
    all_to_all x1, blocking collectives, body(): lax.all_to_all(grad_blocks.reshape(group_rows, 3, 1, group_width), 'head'...  77.7 us
    all_gather x1, waiting for transfers between devices, body(): lax.all_gather(low_qkv, 'dp', axis=0, tiled=True)  69.5 us
    reduce_scatter x1, waiting for transfers between devices, body(): lax.psum_scatter(grad_out, 'dp', scatter_dimension=0, tiled=True)  65.3 us
    unnamed x12, waiting for transfers between devices  60.5 us
    psum x1, waiting for transfers between devices, body(): lax.psum(shard_out.astype(jnp.bfloat16), 'head').astype(jnp.float32)  50.4 us
  transfers between devices with their start and end apart: 14, of which 11 were waited for; matrix products, arithmetic and copies ran while one was open for 15% of the time, Pallas kernels for 0%

profile of v1, /device:TPU:0, one launch (start us, length us, event | category | flops | bytes accessed | tf_op | source)
XLA Modules:
  0.0 1537.1 jit_solution(1415376190136189389)
XLA Ops:
  9.2 69.5 %all-gather.8.cloned.1.call-done = bf16[768,2304]{1,0:T(8,128)(2,1)} async-done(((bf16[96,2304]{1,0:T(8,128)(2,1)}), bf16[768,2304]{1,0:T(8,128)(2,1)}) %all-gather.8.cloned.1.call-update) | async-done | bytes 3538960 | tf_op jit(solution)/shard_map/all_gather | solution.py:107
  78.7 7.1 convolution_convert_fusion
  85.8 4.5 copy.107
  92.4 3.7 all-to-all-start
  102.7 34.5 %all-to-all-done = bf16[768,3,4,192]{0,3,1,2:T(8,128)(2,1)S(1)} async-done(((bf16[768,3,4,192]{0,3,1,2:T(8,128)(2,1)}), bf16[768,3,4,192]{0,3,1,2:T(8,128)(2,1)S(1)}, u32[]{:S(2)}, u32[]{:S(2)}) %all-to-all-start) | async-done | bytes 3538976 | tf_op jit(solution)/shard_map/all_to_all | solution.py:120
  137.2 4.6 copy.109
  141.8 10.9 reshape.363
  152.7 3.7 copy.110
  156.5 45.1 %while.22 = (s32[]{:T(128)}, bf16[3,1024,192]{1,2,0:T(8,128)(2,1)}, f32[3,3,1024]{2,1,0:T(4,128)}, bf16[3,1024,3,3,64]{1,4,3,2,0:T(8,128)(2,1)S(1)}, s32[3,1024]{1,0:T(4,128)S(1)}, /*index=5*/f32[3]{0:T(128)}, s32[]{:T(128)}) while((s32[]{:T(128)}, bf16[3,1024,192]{1,2,0:T(8,128)(2,1)}, f32[3,3,1024]{2,1,0:T(4,128)}, ...), condition=%wide.region_3.4_spmd, body=%wide.region_0.3_spmd.sunk | while | flops 865269760 | bytes 63571132 | solution.py:149
  157.7 3.4 fusion.115
  161.1 3.9 fusion.116
  165.0 5.1 fusion.117
  172.7 3.4 fusion.115
  176.2 3.9 fusion.116
  180.1 5.1 fusion.117
  187.8 3.5 fusion.115
  191.2 3.9 fusion.116
  195.1 5.1 fusion.117
  204.1 10.0 reshape.380
  214.6 19.5 %reduce.13 = bf16[3072,192]{1,0:T(8,128)(2,1)} reduce(bf16[3072,1,192]{2,1,0:T(2,128)(2,1)} %reshape.380, bf16[]{:T(256)} %broadcast.241), dimensions={1}, to_apply=%reshape.380.reduce_sub_computation | reduce | bytes 2359298 | tf_op jit(solution)/shard_map/reshape | solution.py:151
  234.1 4.4 reshape.391
  238.5 4.3 all-to-all-start.1
  249.8 26.1 %all-gather.1 = bf16[8,96,6]{1,2,0:T(8,128)(2,1)S(1)} all-gather(bf16[1,96,6]{1,2,0:T(8,128)(2,1)S(1)} %convert_bitcast_fusion), channel_id=1, replica_groups=mesh['dp'=8,'head'=4] {'dp'}, dimensions={0}, use_global_device_ids=true | all-gather | bytes 10368 | tf_op jit(solution)/shard_map/all_gather | solution.py:111
  279.5 4.7 reshape.392
  284.3 7.3 copy.113
  291.5 3.5 all_to_all.48
  303.0 11.6 fusion.63
  314.6 6.8 copy-done
  321.4 21.9 %multiply_convert_fusion.1 = (bf16[768,3072]{1,0:T(8,128)(2,1)}, f32[768,3072]{1,0:T(8,128)}) fusion(f32[768,6144]{1,0:T(8,128)S(1)} %fusion.63), kind=kLoop, calls=%fused_computation.51 | loop fusion | flops 155713536 | bytes 33030144 | tf_op jit(solution)/shard_map/convert_element_type | solution.py:165
  343.3 17.2 %all-gather.14.cloned.1.call-done = bf16[3072,768]{1,0:T(8,128)(2,1)} async-done(((bf16[384,768]{1,0:T(8,128)(2,1)}), bf16[3072,768]{1,0:T(8,128)(2,1)}) %all-gather.14.cloned.1.call-update) | async-done | bytes 4718608 | tf_op jit(solution)/shard_map/all_gather | solution.py:110
  360.5 9.0 fusion.84
  375.1 19.0 %fusion.28 = (f32[768,3072]{1,0:T(8,128)}, f32[768,3072]{1,0:T(8,128)}) fusion(f32[768,3072]{1,0:T(8,128)} %get-tuple-element.293, f32[768,6144]{1,0:T(8,128)} %copy-done, bf16[3072,768]{1,0:T(8,128)(2,1)} %all-gather.14.cloned.1.call-done, f32[768,768]{0,1:T(8,128)} %get-tuple-element.291, f32[768]{0:T(1024)S(1)} %negate_multiply_fusion.2), kind=kOutput, calls=%fused_computation.75 | convolution fusion | flops 3662807040 | bytes 54266880 | tf_op jit(solution)/shard_map/dot_general | solution.py:47
  394.1 19.8 %multiply_reduce_fusion.1 = (f32[768]{0:T(1024)}, f32[768]{0:T(1024)}, f32[768]{0:T(1024)}, f32[768,768]{0,1:T(8,128)}) fusion(f32[768,768]{0,1:T(8,128)} %copy-done.3, f32[768]{0:T(1024)S(1)} %fusion.58, f32[768]{0:T(1024)S(1)} %broadcast_multiply_fusion.1, f32[768]{0:T(1024)S(1)} %get-tuple-element.237, ...), kind=kOutput, calls=%fused_computation.87 | convolution fusion | flops 7263089664 | bytes 35410944 | tf_op jit(solution)/shard_map/dot_general | solution.py:47
  419.9 4.3 all-to-all-start.2
  424.2 15.9 %all-to-all-done.2 = bf16[768,4,192]{0,2,1:T(8,128)(2,1)} async-done(((bf16[768,4,192]{0,2,1:T(8,128)(2,1)}), bf16[768,4,192]{0,2,1:T(8,128)(2,1)}, u32[]{:S(2)}, u32[]{:S(2)}) %all-to-all-start.2) | async-done | bytes 1179680 | tf_op jit(solution)/shard_map/all_to_all | solution.py:183
  443.3 4.5 reshape.368
  450.7 95.0 %while.23 = (s32[]{:T(128)}, bf16[3,1024,3,192]{1,3,2,0:T(8,128)(2,1)}, bf16[3,1024,3,3,64]{1,4,3,2,0:T(8,128)(2,1)S(1)}, s32[3,1024]{1,0:T(4,128)}, f32[3]{0:T(...) while((s32[]{:T(128)}, bf16[3,1024,3,192]{1,3,2,0:T(8,128)(2,1)}, ...), condition=%wide.region_14.15_spmd, body=%wide.region_12.14_spmd.sunk | while | flops 2055534592 | bytes 141906608 | solution.py:221
  456.4 8.2 multiply_reduce_fusion.6
  464.6 6.7 fusion.124
  471.3 6.6 multiply_convert_fusion.3
  488.0 8.2 multiply_reduce_fusion.6
  496.2 6.7 fusion.124
  503.0 6.6 multiply_convert_fusion.3
  519.7 8.2 multiply_reduce_fusion.6
  527.9 6.7 fusion.124
  534.7 6.6 multiply_convert_fusion.3
  545.7 9.8 copy.136
  555.5 77.7 %all_to_all.60 = bf16[3072,3,1,192]{3,1,2,0:T(4,128)(2,1)} all-to-all(bf16[3072,3,1,192]{3,1,2,0:T(4,128)(2,1)} %bitcast.156), channel_id=1, replica_groups=mesh['dp'=8,'head'=4] {'head'}, dimensions={0} | all-to-all | bytes 7077888 | tf_op jit(solution)/shard_map/all_to_all | solution.py:222
  633.3 10.5 copy.137
  646.2 5.0 convolution_bitcast_fusion
  651.1 8.1 copy.138
  670.1 8.8 fusion.47
  680.5 20.6 %fusion.39 = f32[768,6144]{1,0:T(8,128)} fusion(f32[768,3072]{1,0:T(8,128)} %get-tuple-element.299, f32[768,3072]{1,0:T(8,128)} %get-tuple-element.298, f32[768,768]{0,1:T(8,128)S(1)} %copy-done.4, f32[768]{0:T(1024)S(1)} %copy-done.34, f32[768]{0:T(1024)S(1)} %copy-done.32, f32[768]{0:T(1024)S(1)} %copy-done.30, f32[768]{0:T(1024)S(1)} %copy-done.26), kind=kOutput, calls=%fused_computation.107 | convolution fusion | flops 7260143616 | bytes 40120320 | tf_op jit(solution)/shard_map/dot_general | solution.py:41
  701.3 84.4 %reduce-scatter.16.cloned.1.call-done = f32[96,2304]{1,0:T(8,128)} async-done(((f32[768,2304]{1,0:T(8,128)}), f32[96,2304]{1,0:T(8,128)}) %reduce-scatter.16.cloned.1.call-update) | async-done | bytes 884752 | tf_op jit(solution)/shard_map/reduce_scatter | solution.py:243
  789.9 60.4 %reduce-scatter.18.cloned.1.call-done = f32[96,6]{1,0:T(8,128)} async-done(((f32[768,6]{1,0:T(8,128)}), f32[96,6]{1,0:T(8,128)}) %reduce-scatter.18.cloned.1.call-update) | async-done | bytes 2320
  851.1 5.8 psum.38
  857.5 65.3 %reduce-scatter.10.cloned.1.call-done = f32[96,768]{1,0:T(8,128)} async-done(((f32[768,768]{1,0:T(8,128)}), f32[96,768]{1,0:T(8,128)}) %reduce-scatter.10.cloned.1.call-update) | async-done | bytes 294928 | tf_op jit(solution)/shard_map/reduce_scatter | solution.py:244
  924.4 164.8 %reduce-scatter.14.cloned.1.call-done = f32[384,768]{1,0:T(8,128)} async-done(((f32[3072,768]{1,0:T(8,128)}), f32[384,768]{1,0:T(8,128)}) %reduce-scatter.14.cloned.1.call-update) | async-done | bytes 1179664 | tf_op jit(solution)/shard_map/reduce_scatter | solution.py:246
  1091.3 314.6 %reduce-scatter.12.cloned.1.call-done = f32[96,6144]{1,0:T(8,128)} async-done(((f32[768,6144]{1,0:T(8,128)}), f32[96,6144]{1,0:T(8,128)}) %reduce-scatter.12.cloned.1.call-update) | async-done | bytes 2359312 | tf_op jit(solution)/shard_map/reduce_scatter | solution.py:245
  1408.8 7.4 add_add_fusion.4
  1416.2 11.8 all-gather.16.cloned.1.call-done
  1430.6 50.4 %all-reduce.5.cloned.1.call-done = (bf16[96,768]{1,0:T(8,128)(2,1)}, bf16[96,6144]{1,0:T(8,128)(2,1)}, bf16[384,768]{1,0:T(8,128)(2,1)}) async-done(((bf16[96,768]{1,0:T(8,128)(2,1)}, bf16[96,6144]{1,0:T(8,128)(2,1)}, bf16[384,768]{1,0:T(8,128)(2,1)}), (bf16[96,768]{1,0:T(8,128)(2,1)}, bf16[96,6144]{1,0:T(8,128)(2,1)}, bf16[384,768]{1,0:T(8,128)(2,1)})) %all-reduce.5.cloned.1.call-update) | async-done | bytes 1916944 | tf_op jit(solution)/shard_map/psum | solution.py:251
  1493.5 21.8 %psum.39 = f32[]{:T(128)} all-reduce(f32[]{:T(128)S(6)} %add.229), channel_id=1, replica_groups=mesh['dp'=8,'head'=4] {'dp'}, use_global_device_ids=true, to_apply=%region_36.37 | all-reduce | flops 1 | bytes 8 | tf_op jit(solution)/shard_map/psum | solution.py:259
  1521.2 4.7 fusion.71
  (264 shorter events, 134.4 us)
Async XLA Ops:
  7.2 71.5 %all-gather.8.cloned.1.call-start = ((), (), s32[]{:S(2)}) async-start(), calls=%async_computation.9 | async-start | bytes 3981312 | tf_op jit(solution)/shard_map/all_gather | solution.py:107
  92.4 44.9 %all-to-all-start = ((bf16[768,3,4,192]{0,3,1,2:T(8,128)(2,1)}), bf16[768,3,4,192]{0,3,1,2:T(8,128)(2,1)S(1)}, u32[]{:S(2)}, u32[]{:S(2)}) async-start(bf16[768,3,4,192]{0,3,1,2:T(8,128)(2,1)} %copy.108), calls=%async_computation | async-start | bytes 7077888 | tf_op jit(solution)/shard_map/all_to_all | solution.py:120
  96.1 201.3 %all-gather.10.cloned.1.call-start = ((), (), s32[]{:S(2)}) async-start(), calls=%async_computation.10 | async-start | bytes 1327104 | tf_op jit(solution)/shard_map/all_gather | solution.py:108
  97.8 205.1 %all-gather.12.cloned.1.call-start = ((), (), s32[]{:S(2)}) async-start(), calls=%async_computation.11 | async-start | bytes 10616832 | tf_op jit(solution)/shard_map/all_gather | solution.py:109
  201.6 12.5 copy-start.36
  238.5 41.1 %all-to-all-start.1 = ((bf16[4,2,73728]{2,1,0:T(2,128)(2,1)}), bf16[4,2,73728]{2,1,0:T(2,128)(2,1)}, u32[]{:S(2)}, u32[]{:S(2)}) async-start(bf16[4,2,73728]{2,1,0:T(2,128)(2,1)} %reshape.391), calls=%async_computation.1 | async-start | bytes 2359296 | tf_op jit(solution)/shard_map/all_to_all | solution.py:150
  242.8 117.7 %all-gather.14.cloned.1.call-start = ((), (), s32[]{:S(2)}) async-start(), calls=%async_computation.12 | async-start | bytes 5308416 | tf_op jit(solution)/shard_map/all_gather | solution.py:110
  245.0 4.8 copy-start.49
  279.5 80.9 %copy-start.33 = (f32[768]{0:T(1024)}, f32[768]{0:T(1024)S(1)}, u32[]{:S(2)}) copy-start(f32[768]{0:T(1024)S(1)} %get-tuple-element.236) | copy-start | bytes 9220
  279.5 135.0 %copy-start.31 = (f32[768]{0:T(1024)}, f32[768]{0:T(1024)S(1)}, u32[]{:S(2)}) copy-start(f32[768]{0:T(1024)S(1)} %get-tuple-element.237) | copy-start | bytes 9220
  300.7 113.9 %copy-start.25 = (f32[768]{0:T(1024)}, f32[768]{0:T(1024)S(1)}, u32[]{:S(2)}) copy-start(f32[768]{0:T(1024)S(1)} %broadcast_multiply_fusion.1) | copy-start | bytes 9220
  303.0 111.6 %copy-start.29 = (f32[768]{0:T(1024)}, f32[768]{0:T(1024)S(1)}, u32[]{:S(2)}) copy-start(f32[768]{0:T(1024)S(1)} %fusion.58) | copy-start | bytes 9220
  314.6 6.8 copy-start
  369.8 2.6 copy-start.48
  375.1 19.0 %copy-start.46 = (f32[768]{0:T(1024)}, f32[768]{0:T(1024)S(1)}, u32[]{:S(2)}) copy-start(f32[768]{0:T(1024)S(1)} %negate_multiply_fusion.2) | copy-start | bytes 9220
  394.1 19.8 %copy-start.41 = (f32[768]{0:T(1024)S(1)}, f32[768]{0:T(1024)}, u32[]{:S(2)}) copy-start(f32[768]{0:T(1024)} %copy-done.40) | copy-start | bytes 9220
  414.6 3.1 copy-start.55
  417.7 2.2 copy-start.7
  417.7 2.2 copy-start.44
  419.9 20.2 %all-to-all-start.2 = ((bf16[768,4,192]{0,2,1:T(8,128)(2,1)}), bf16[768,4,192]{0,2,1:T(8,128)(2,1)}, u32[]{:S(2)}, u32[]{:S(2)}) async-start(bf16[768,4,192]{0,2,1:T(8,128)(2,1)} %bitcast.169), calls=%async_computation.2 | async-start | bytes 2359296 | tf_op jit(solution)/shard_map/all_to_all | solution.py:183
  424.2 361.5 %reduce-scatter.16.cloned.1.call-start = ((), (), s32[]{:S(2)}) async-start(), calls=%async_computation.17 | async-start | bytes 7962624 | tf_op jit(solution)/shard_map/reduce_scatter | solution.py:243
  443.3 7.4 copy-start.38
  450.7 3.2 copy-start.1
  480.0 2.3 copy-start.2
  482.3 3.2 copy-start.1
  511.6 2.4 copy-start.2
  514.0 3.2 copy-start.1
  543.3 2.4 copy-start.2
  643.8 2.4 copy-start.21
  644.3 1.9 copy-start.15
  659.2 1.9 copy-start.8
  659.2 1.9 copy-start.45
  659.3 2.6 copy-start.47
  659.3 190.9 %reduce-scatter.18.cloned.1.call-start = ((), (), s32[]{:S(2)}) async-start(), calls=%async_computation.18 | async-start | bytes 442368
  659.3 2.6 copy-start.10
  661.1 4.8 copy-start.22
  665.8 257.0 %reduce-scatter.10.cloned.1.call-start = ((), (), s32[]{:S(2)}) async-start(), calls=%async_computation.13 | async-start | bytes 2654208 | tf_op jit(solution)/shard_map/reduce_scatter | solution.py:244
  668.4 420.7 %reduce-scatter.14.cloned.1.call-start = ((), (), s32[]{:S(2)}) async-start(), calls=%async_computation.15 | async-start | bytes 10616832 | tf_op jit(solution)/shard_map/reduce_scatter | solution.py:246
  678.8 1.7 copy-start.4
  678.8 1.7 copy-start.26
  678.8 1.7 copy-start.30
  678.8 1.7 copy-start.32
  678.8 1.7 copy-start.34
  678.9 727.1 %reduce-scatter.12.cloned.1.call-start = ((), (), s32[]{:S(2)}) async-start(), calls=%async_computation.14 | async-start | bytes 21233664 | tf_op jit(solution)/shard_map/reduce_scatter | solution.py:245
  701.2 87.2 %copy-start.14 = (bf16[768,768]{0,1:T(8,128)(2,1)S(1)}, bf16[768,768]{0,1:T(8,128)(2,1)}, u32[]{:S(2)}) copy-start(bf16[768,768]{0,1:T(8,128)(2,1)} %get-tuple-element.300) | copy-start | bytes 3538948
  701.2 726.8 %all-gather.16.cloned.1.call-start = ((), (), s32[]{:S(2)}) async-start(), calls=%async_computation.16 | async-start | bytes 2211840 | tf_op jit(solution)/shard_map/all_gather | solution.py:25
  787.7 693.2 %all-reduce.5.cloned.1.call-start = ((), (), s32[]{:S(2)}) async-start(), calls=%async_computation.19 | async-start | bytes 3833856 | tf_op jit(solution)/shard_map/psum | solution.py:251
  1091.3 317.5 %copy-start.9 = (f32[768,768]{0,1:T(8,128)S(1)}, f32[768,768]{0,1:T(8,128)}, u32[]{:S(2)}) copy-start(f32[768,768]{0,1:T(8,128)} %copy-done.7) | copy-start | bytes 7077892
  1490.2 25.8 %copy-start.16 = (f32[96,2304]{1,0:T(8,128)S(1)}, f32[96,2304]{1,0:T(8,128)}, u32[]{:S(2)}) copy-start(f32[96,2304]{1,0:T(8,128)} %param.28) | copy-start | bytes 2654212
  1490.2 25.8 %copy-start.27 = (f32[96,2304]{1,0:T(8,128)S(1)}, f32[96,2304]{1,0:T(8,128)}, u32[]{:S(2)}) copy-start(f32[96,2304]{1,0:T(8,128)} %param.33) | copy-start | bytes 2654212
  1490.2 25.8 %copy-start.28 = (f32[96,2304]{1,0:T(8,128)S(1)}, f32[96,2304]{1,0:T(8,128)}, u32[]{:S(2)}) copy-start(f32[96,2304]{1,0:T(8,128)} %param.38) | copy-start | bytes 2654212
  1490.2 28.0 %copy-start.20 = (f32[96,768]{1,0:T(8,128)S(1)}, f32[96,768]{1,0:T(8,128)}, u32[]{:S(2)}) copy-start(f32[96,768]{1,0:T(8,128)} %param.29) | copy-start | bytes 884740
  1490.3 28.0 %copy-start.35 = (bf16[96,768]{1,0:T(8,128)(2,1)S(1)}, bf16[96,768]{1,0:T(8,128)(2,1)}, u32[]{:S(2)}) copy-start(bf16[96,768]{1,0:T(8,128)(2,1)} %get-tuple-element.265) | copy-start | bytes 442372
  1516.1 5.1 copy-start.6
  1516.1 5.1 copy-start.17
  1516.1 5.1 copy-start.18
  1518.2 3.0 copy-start.12
  1521.2 4.8 copy-start.13
  1521.2 4.8 copy-start.19
  1521.2 4.8 copy-start.23
  1521.2 4.7 copy-start.24
  1526.0 2.7 copy-start.50
  1526.0 2.7 copy-start.51
  1526.0 2.7 copy-start.52
  (12 other events, 12.1 us)
Sparse Core Ops, SparseCore 0:
  10.8 67.8 all-gather.7
  99.7 40.1 all-gather.9
  142.7 136.8 all-gather.11
  282.1 78.2 all-gather.13
  659.4 126.2 reduce-scatter.15
  789.7 60.4 reduce-scatter.17
  854.7 68.0 reduce-scatter.9
  926.8 162.3 reduce-scatter.13
  1093.6 312.3 reduce-scatter.11
  1408.0 19.8 all-gather.15
  1431.9 49.0 all-reduce.4
